TPU v7x, 32 devices: a whole 2x2x4 slice. The times are simulated.
32 devices in a mesh: nodes: 8 (over y, x, core), cols: 4 (over z).
Axes of the slice: x: 2, y: 2, z: 4, core: 2. Of those that a mesh axis runs over, the one named last changes fastest.
Arguments:
- features: bfloat16 [1024, 512], P('nodes', 'cols'), may hold values from -6 to 6
- weight: bfloat16 [512, 512], P(None, 'cols'), may hold values from -0.25 to 0.25
- degree: int32 [1024], P('nodes'), may hold values from 1 to 64
- tile_cols: int32 [8, 8], P('nodes'), may hold values from 0 to 7, as said below
- tile_count: int32 [8], P('nodes'), may hold values from 1 to 8, as said below
- tile_codes: int32 [8, 8], P('nodes'), may hold values from 0 to 1048575
- cotangent: bfloat16 [1024, 512], P('nodes', 'cols'), may hold values from -6 to 6
Outputs:
- activation: bfloat16 [1024, 512], P('nodes', 'cols')
- weight_grad: float32 [512, 512], P(None, 'cols')
- feats_grad: float32 [1024, 512], P('nodes', 'cols')
Inputs may be any that keep to these rules, and one draw needn't show every extreme that they name: `tile_cols`: each row lists every node block once, and row i begins with block i. The tiles of row block i are those of its first tile_count[i] slots; some row block holds all 8.
All inputs are finite; a program needn't handle non-finite values.
Results may differ from a plain program's by a relative error of at most 0.0065.
Values may be sent and summed in bfloat16 or wider, within the bound.
A program may use at most 64 MiB of HBM per device.

v0:
```python
import jax
import jax.numpy as jnp
from jax import lax
from jax.sharding import PartitionSpec as P

TILE = 128


def tile_bits(pattern_code):
    line_ids = jnp.arange(TILE, dtype=jnp.int32)
    hashed = (
        pattern_code[..., None, None] * 73856093
        ^ line_ids[:, None] * 19349663
        ^ line_ids[None, :] * 83492791
    )
    hashed = hashed ^ hashed >> 13
    hashed = hashed * 1274126177
    hashed = hashed ^ hashed >> 16
    return hashed & 63 == 0


def make_tiles(matches, code_table, live_limit, own, identity):
    slot_ids = jnp.arange(matches.shape[1], dtype=jnp.int32)
    slot_index = jnp.sum(jnp.where(matches, slot_ids[None, :], 0), axis=1, dtype=jnp.int32)
    code_value = jnp.sum(jnp.where(matches, code_table, 0), axis=1, dtype=jnp.int32)
    pattern = tile_bits(code_value) & (slot_index < live_limit)[:, None, None]
    values = (
        pattern.astype(jnp.float32)
        + jnp.where(own, 1.0, 0.0).astype(jnp.float32)[:, None, None] * identity
    )
    return values.astype(jnp.bfloat16)


def body(features, weight, degree, tile_cols, tile_count, tile_codes, cotangent):
    my_block = lax.axis_index("nodes")
    identity = jnp.eye(TILE, dtype=jnp.float32)
    inv_root = lax.rsqrt(degree.astype(jnp.float32))[:, None]
    scaled = (features.astype(jnp.float32) * inv_root).astype(jnp.bfloat16)
    my_cols = tile_cols[0]
    my_codes = tile_codes[0]
    my_count = tile_count[0]
    pieces = lax.all_gather(scaled[None], "nodes", axis=0, tiled=True)
    count_blocks = pieces.shape[0]
    targets = jnp.arange(count_blocks, dtype=jnp.int32)
    matches = targets[:, None] == my_cols[None, :]
    tiles = make_tiles(matches, my_codes[None, :], my_count, targets == my_block, identity)
    gathered = lax.dot_general(
        tiles, pieces, (((0, 2), (0, 1)), ((), ())), preferred_element_type=jnp.float32
    )
    aggregated = (inv_root * gathered).astype(jnp.bfloat16)
    agg_full = lax.all_gather(aggregated, "cols", axis=1, tiled=True)
    pre = jnp.dot(agg_full, weight, preferred_element_type=jnp.float32)
    activation = jax.nn.silu(pre).astype(jnp.bfloat16)
    sigma = jax.nn.sigmoid(pre)
    grad_pre = (cotangent.astype(jnp.float32) * sigma * (1.0 + pre * (1.0 - sigma))).astype(
        jnp.bfloat16
    )
    partial_grad = lax.dot_general(
        agg_full, grad_pre, (((0,), (0,)), ((), ())), preferred_element_type=jnp.float32
    )
    weight_grad = lax.psum(partial_grad, "nodes")
    terms = lax.dot_general(
        grad_pre, weight, (((1,), (1,)), ((), ())), preferred_element_type=jnp.float32
    )
    grad_agg = lax.psum_scatter(terms, "cols", scatter_dimension=1, tiled=True)
    grad_scaled = (inv_root * grad_agg).astype(jnp.bfloat16)
    all_cols, all_counts, all_codes = (
        lax.all_gather(tile_cols, "nodes", axis=0, tiled=True),
        lax.all_gather(tile_count, "nodes", axis=0, tiled=True),
        lax.all_gather(tile_codes, "nodes", axis=0, tiled=True),
    )
    pieces = lax.all_gather(grad_scaled[None], "nodes", axis=0, tiled=True)
    count_blocks = pieces.shape[0]
    row_ids = jnp.arange(count_blocks, dtype=jnp.int32)
    tiles = make_tiles(all_cols == my_block, all_codes, all_counts, row_ids == my_block, identity)
    back_total = lax.dot_general(
        tiles, pieces, (((0, 1), (0, 1)), ((), ())), preferred_element_type=jnp.float32
    )
    feats_grad = inv_root * back_total
    return (activation, weight_grad, feats_grad)


def solution(mesh):
    in_specs = (
        P("nodes", "cols"),
        P(None, "cols"),
        P("nodes"),
        P("nodes", None),
        P("nodes"),
        P("nodes", None),
        P("nodes", "cols"),
    )
    out_specs = (P("nodes", "cols"), P(None, "cols"), P("nodes", "cols"))
    return jax.shard_map(body, mesh=mesh, in_specs=in_specs, out_specs=out_specs, check_vma=False)
```

profile of v0, /device:TPU:0, one launch (start us, length us, event | category | flops | bytes accessed | tf_op | source)
XLA Modules:
  0.0 118.2 jit_solution(6654077568115102820)
XLA Ops:
  8.0 0.0 copy-start
  8.0 0.0 reduce-scatter.2.cloned.1.call-start
  8.1 0.0 copy-start.2
  8.1 0.0 copy-start.4
  8.1 0.6 copy-done.4
  8.8 10.2 %all-gather.2 = s32[8,1,8]{2,1,0:T(1,128)S(1)} all-gather(s32[1,1,8]{2,1,0:T(1,128)S(1)} %bitcast.36), channel_id=1, replica_groups=mesh['nodes'=8,'cols'=4] {'nodes'}, dimensions={0}, use_global_device_ids=true | all-gather | bytes 288 | tf_op jit(solution)/shard_map/all_gather | solution.py:68
  19.0 0.7 copy-done.3
  19.6 8.8 %all-gather.3 = s32[8,1,8]{2,1,0:T(1,128)S(1)} all-gather(s32[1,1,8]{2,1,0:T(1,128)S(1)} %bitcast.34), channel_id=1, replica_groups=mesh['nodes'=8,'cols'=4] {'nodes'}, dimensions={0}, use_global_device_ids=true | all-gather | bytes 288 | tf_op jit(solution)/shard_map/all_gather | solution.py:70
  28.5 0.1 multiply_convert_fusion.3
  28.6 8.3 %all-gather = bf16[1024,128]{1,0:T(8,128)(2,1)S(1)} all-gather(bf16[128,128]{1,0:T(8,128)(2,1)S(1)} %multiply_convert_fusion.3), channel_id=2, replica_groups=mesh['nodes'=8,'cols'=4] {'nodes'}, dimensions={0}, use_global_device_ids=true | all-gather | bytes 294912 | tf_op jit(solution)/shard_map/all_gather | solution.py:42
  37.6 0.1 select_reduce_fusion
  37.7 0.2 select_reduce_fusion.2
  37.9 0.1 broadcast_xor_fusion
  38.0 0.5 fusion.2
  38.5 12.5 %all_gather.19 = bf16[128,512]{1,0:T(8,128)(2,1)S(1)} all-gather(bf16[128,128]{1,0:T(8,128)(2,1)S(1)} %fusion.2), channel_id=1, replica_groups=mesh['nodes'=8,'cols'=4] {'cols'}, dimensions={1}, use_global_device_ids=true | all-gather | bytes 163840 | tf_op jit(solution)/shard_map/all_gather | solution.py:51
  51.0 0.8 multiply_convert_fusion.2
  51.8 0.9 fusion.46
  52.7 0.0 reduce-scatter.2.cloned.1.call-update
  52.7 0.0 all-reduce.3.cloned.1.call-start
  52.7 0.0 copy-start.6
  52.8 0.6 copy-done.6
  53.4 0.6 dynamic-slice
  54.0 0.8 dynamic-update-slice
  54.7 0.9 fusion.47
  55.7 0.0 all-reduce.3.cloned.1.call-update
  55.7 7.4 %all-reduce = s32[8]{0:T(128)S(1)} all-reduce(s32[8]{0:T(128)S(1)} %dynamic-update-slice), channel_id=1, replica_groups=mesh['nodes'=8,'cols'=4] {'nodes'}, use_global_device_ids=true, to_apply=%add | all-reduce | flops 8 | bytes 64
  63.1 8.6 %reduce-scatter.2.cloned.1.call-done = f32[128,128]{1,0:T(8,128)} async-done(((f32[128,512]{1,0:T(8,128)}), f32[128,128]{1,0:T(8,128)}) %reduce-scatter.2.cloned.1.call-update) | async-done | bytes 65552 | tf_op jit(solution)/shard_map/reduce_scatter | solution.py:65
  71.7 0.9 multiply_convert_fusion
  72.6 9.5 %all-gather.1 = bf16[1024,128]{1,0:T(8,128)(2,1)S(1)} all-gather(bf16[128,128]{1,0:T(8,128)(2,1)S(1)} %multiply_convert_fusion), channel_id=3, replica_groups=mesh['nodes'=8,'cols'=4] {'nodes'}, dimensions={0}, use_global_device_ids=true | all-gather | bytes 294912 | tf_op jit(solution)/shard_map/all_gather | solution.py:72
  82.1 1.1 fusion
  83.1 26.0 %all-reduce.3.cloned.1.call-done = f32[512,128]{1,0:T(8,128)} async-done(((f32[512,128]{1,0:T(8,128)}), f32[512,128]{1,0:T(8,128)}) %all-reduce.3.cloned.1.call-update) | async-done | bytes 262160 | tf_op jit(solution)/shard_map/psum | solution.py:61
  109.1 1.7 %copy.18 = f32[512,128]{1,0:T(8,128)} copy(f32[512,128]{1,0:T(8,128)} %all-reduce.3.cloned.1.call-done) | data formatting | bytes 524288
  (16 shorter events, 0.1 us)
Async XLA Ops:
  8.0 43.0 %copy-start = (bf16[512,128]{1,0:T(8,128)(2,1)S(1)}, bf16[512,128]{1,0:T(8,128)(2,1)}, u32[]{:S(2)}) copy-start(bf16[512,128]{1,0:T(8,128)(2,1)} %param.8) | copy-start | bytes 393220
  8.0 63.7 %reduce-scatter.2.cloned.1.call-start = ((), (), s32[]{:S(2)}) async-start(), calls=%async_computation.2 | async-start | bytes 327680 | tf_op jit(solution)/shard_map/reduce_scatter | solution.py:65
  8.1 20.4 %copy-start.2 = (bf16[128,128]{1,0:T(8,128)(2,1)S(1)}, bf16[128,128]{1,0:T(8,128)(2,1)}, u32[]{:S(2)}) copy-start(bf16[128,128]{1,0:T(8,128)(2,1)} %param.7) | copy-start | bytes 98308
  8.1 0.7 copy-start.4
  19.0 0.7 copy-start.3
  19.6 8.8 %copy-start.5 = (s32[128]{0:T(128)S(1)}, s32[128]{0:T(128)}, u32[]{:S(2)}) copy-start(s32[128]{0:T(128)} %param.9) | copy-start | bytes 1540
  51.0 0.8 copy-start.1
  52.7 56.4 %all-reduce.3.cloned.1.call-start = ((), (), s32[]{:S(2)}) async-start(), calls=%async_computation.1 | async-start | bytes 524288 | tf_op jit(solution)/shard_map/psum | solution.py:61
  52.7 0.7 copy-start.6
Sparse Core Ops, SparseCore 0:
  52.8 18.8 reduce-scatter.1
Sparse Core Ops, SparseCore 1:
  56.8 52.3 all-reduce.2
where the time goes:
time: 119 us; the launch traced here: 118 us
  blocking collectives  56.7 us (48%)
  waiting for transfers between devices  34.7 us (29%)
  between operations  16.2 us (14%)
  local copies, waits for them, and re-layouts  4.98 us (4%)
  matrix products  4.16 us (3%)
  other arithmetic  1.41 us (1%)
    psum x1, waiting for transfers between devices, body(): weight_grad = lax.psum(partial_grad, 'nodes')  26 us
    all_gather x1, blocking collectives, body(): agg_full = lax.all_gather(aggregated, 'cols', axis=1, tiled=True)  12.5 us
    all_gather x1, blocking collectives, body(): lax.all_gather(tile_cols, 'nodes', axis=0, tiled=True)  10.2 us
    all_gather x1, blocking collectives, body(): pieces = lax.all_gather(grad_scaled[None], 'nodes', axis=0, tiled=True)  9.48 us
    all_gather x1, blocking collectives, body(): lax.all_gather(tile_codes, 'nodes', axis=0, tiled=True)  8.84 us
    reduce_scatter x1, waiting for transfers between devices, body(): grad_agg = lax.psum_scatter(terms, 'cols', scatter_dimension=1, tiled=True)  8.63 us
    all_gather x1, blocking collectives, body(): pieces = lax.all_gather(scaled[None], 'nodes', axis=0, tiled=True)  8.34 us
    unnamed x1, blocking collectives  7.36 us
  transfers between devices with their start and end apart: 2, of which 2 were waited for; matrix products, arithmetic and copies ran while one was open for 4% of the time, Pallas kernels for 0%

commit v1 on v0

--- a/solution.py
+++ b/solution.py
@@ -58,7 +58,8 @@
     partial_grad = lax.dot_general(
         agg_full, grad_pre, (((0,), (0,)), ((), ())), preferred_element_type=jnp.float32
     )
-    weight_grad = lax.psum(partial_grad, "nodes")
+    parts = lax.all_gather(partial_grad, "nodes")
+    weight_grad = jnp.sum(parts, axis=0)
     terms = lax.dot_general(
         grad_pre, weight, (((1,), (1,)), ((), ())), preferred_element_type=jnp.float32
     )

time: 119 us -> 94.8 us (0.80)
  waiting for transfers between devices: 34.7 us -> 9.26 us
  other arithmetic: 1.41 us -> 5.92 us
  local copies, waits for them, and re-layouts: 4.98 us -> 1.46 us
    psum x1 -> x0, waiting for transfers between devices: 26 us -> none  [body(): weight_grad = lax.psum(partial_grad, 'nodes')]
    unnamed x18 -> x9, local copies, waits for them, and re-layouts: 4.98 us -> 1.46 us
    reduce_sum x0 -> x1, other arithmetic: none -> 2.42 us  [body(): weight_grad = jnp.sum(parts, axis=0)]
    all_gather x1, blocking collectives: 10.2 us -> 8.6 us  [body(): lax.all_gather(tile_cols, 'nodes', axis=0, tiled=True)]
    all_gather x1, blocking collectives: 8.84 us -> 10.3 us  [body(): lax.all_gather(tile_codes, 'nodes', axis=0, tiled=True)]
  transfers between devices with their start and end apart: 2 -> 2, of which waited for: 2 -> 1; matrix products, arithmetic and copies ran while one was open for 4% -> 5% of each run, Pallas kernels for 0% -> 0%
where the time goes in v1:
time: 94.8 us; the launch traced here: 94.4 us
  blocking collectives  57.3 us (60%)
  between operations  16.2 us (17%)
  waiting for transfers between devices  9.26 us (10%)
  other arithmetic  5.92 us (6%)
  matrix products  4.19 us (4%)
  local copies, waits for them, and re-layouts  1.46 us (2%)
    all_gather x1, blocking collectives, body(): agg_full = lax.all_gather(aggregated, 'cols', axis=1, tiled=True)  12.5 us
    all_gather x1, blocking collectives, body(): lax.all_gather(tile_codes, 'nodes', axis=0, tiled=True)  10.3 us
    all_gather x1, blocking collectives, body(): pieces = lax.all_gather(grad_scaled[None], 'nodes', axis=0, tiled=True)  10.2 us
    reduce_scatter x1, waiting for transfers between devices, body(): grad_agg = lax.psum_scatter(terms, 'cols', scatter_dimension=1, tiled=True)  9.22 us
    all_gather x1, blocking collectives, body(): lax.all_gather(tile_cols, 'nodes', axis=0, tiled=True)  8.6 us
    all_gather x1, blocking collectives, body(): pieces = lax.all_gather(scaled[None], 'nodes', axis=0, tiled=True)  8.45 us
    unnamed x1, blocking collectives  7.24 us
    reduce_sum x1, other arithmetic, body(): weight_grad = jnp.sum(parts, axis=0)  2.42 us
  transfers between devices with their start and end apart: 2, of which 1 were waited for; matrix products, arithmetic and copies ran while one was open for 5% of the time, Pallas kernels for 0%

profile of v1, /device:TPU:0, one launch (start us, length us, event | category | flops | bytes accessed | tf_op | source)
XLA Modules:
  0.0 94.4 jit_solution(12111465652870028881)
XLA Ops:
  8.0 0.0 copy-start
  8.0 0.0 copy-start.1
  8.0 0.0 reduce-scatter.2.cloned.1.call-start
  8.1 10.3 %all-gather.4 = s32[8,1,8]{2,1,0:T(1,128)S(1)} all-gather(s32[1,1,8]{2,1,0:T(1,128)} %bitcast.36), channel_id=1, replica_groups=mesh['nodes'=8,'cols'=4] {'nodes'}, dimensions={0}, use_global_device_ids=true | all-gather | bytes 288 | tf_op jit(solution)/shard_map/all_gather | solution.py:71
  18.4 8.6 %all-gather.3 = s32[8,1,8]{2,1,0:T(1,128)S(1)} all-gather(s32[1,1,8]{2,1,0:T(1,128)} %bitcast.38), channel_id=1, replica_groups=mesh['nodes'=8,'cols'=4] {'nodes'}, dimensions={0}, use_global_device_ids=true | all-gather | bytes 288 | tf_op jit(solution)/shard_map/all_gather | solution.py:69
  27.0 0.7 convert_rsqrt_fusion
  27.7 0.8 multiply_convert_fusion.3
  28.5 0.0 copy-start.2
  28.6 8.4 %all-gather = bf16[1024,128]{1,0:T(8,128)(2,1)S(1)} all-gather(bf16[128,128]{1,0:T(8,128)(2,1)S(1)} %multiply_convert_fusion.3), channel_id=2, replica_groups=mesh['nodes'=8,'cols'=4] {'nodes'}, dimensions={0}, use_global_device_ids=true | all-gather | bytes 294912 | tf_op jit(solution)/shard_map/all_gather | solution.py:42
  37.7 0.1 select_reduce_fusion
  37.8 0.8 select_reduce_fusion.2
  38.6 0.1 broadcast_xor_fusion
  38.7 0.5 fusion.2
  39.2 12.5 %all_gather.25 = bf16[128,512]{1,0:T(8,128)(2,1)S(1)} all-gather(bf16[128,128]{1,0:T(8,128)(2,1)S(1)} %fusion.2), channel_id=1, replica_groups=mesh['nodes'=8,'cols'=4] {'cols'}, dimensions={1}, use_global_device_ids=true | all-gather | bytes 163840 | tf_op jit(solution)/shard_map/all_gather | solution.py:51
  51.7 0.0 copy-done
  51.7 0.8 multiply_convert_fusion.2
  52.5 0.0 copy-done.1
  52.5 0.9 fusion.46
  53.4 0.0 reduce-scatter.2.cloned.1.call-update
  53.5 0.0 all-gather.7.cloned.1.call-start
  53.5 0.9 fusion.47
  54.4 0.0 all-gather.7.cloned.1.call-update
  54.5 0.0 copy-done.2
  54.5 0.7 dynamic-slice
  55.1 0.8 dynamic-update-slice
  55.9 7.2 %all-reduce = s32[8]{0:T(128)S(1)} all-reduce(s32[8]{0:T(128)S(1)} %dynamic-update-slice), channel_id=1, replica_groups=mesh['nodes'=8,'cols'=4] {'nodes'}, use_global_device_ids=true, to_apply=%add | all-reduce | flops 8 | bytes 64
  63.2 9.2 %reduce-scatter.2.cloned.1.call-done = f32[128,128]{1,0:T(8,128)} async-done(((f32[128,512]{1,0:T(8,128)}), f32[128,128]{1,0:T(8,128)}) %reduce-scatter.2.cloned.1.call-update) | async-done | bytes 65552 | tf_op jit(solution)/shard_map/reduce_scatter | solution.py:66
  72.4 0.9 multiply_convert_fusion
  73.3 10.2 %all-gather.2 = bf16[1024,128]{1,0:T(8,128)(2,1)S(1)} all-gather(bf16[128,128]{1,0:T(8,128)(2,1)S(1)} %multiply_convert_fusion), channel_id=4, replica_groups=mesh['nodes'=8,'cols'=4] {'nodes'}, dimensions={0}, use_global_device_ids=true | all-gather | bytes 294912 | tf_op jit(solution)/shard_map/all_gather | solution.py:73
  83.5 1.1 %fusion = f32[128,128]{1,0:T(8,128)} fusion(bf16[8,128,128]{2,1,0:T(8,128)(2,1)S(1)} %bitcast.33, s32[8,128]{1,0:T(8,128)S(1)} %get-tuple-element.7, f32[128,128]{0,1:T(8,128)S(1)} %fusion.35, f32[8]{0:T(128)S(1)} %compare_select_fusion, s32[128]{0:T(128)S(1)} %iota_multiply_fusion, pred[8]{0:T(512)(128)(4,1)S(1)} %lt.15, f32[128]{0:T(128)S(1)} %convert_rsqrt_fusion), kind=kOutput, calls=%fused_computation.1 | convolution fusion | flops 35274752 | bytes 398376 | tf_op jit(solution)/shard_map/dot_general | solution.py:77
  84.5 0.0 all-gather.7.cloned.1.call-done
  84.5 2.4 %reduce_sum.47 = f32[512,128]{1,0:T(8,128)} reduce(f32[8,512,128]{2,1,0:T(8,128)} %bitcast.31, f32[]{:T(128)} %constant.11.clone.1), dimensions={0}, to_apply=%region_2.3 | reduce | flops 458752 | bytes 2359300 | tf_op jit(solution)/shard_map/reduce_sum | solution.py:62
  (8 shorter events, 0.0 us)
Async XLA Ops:
  8.0 43.7 %copy-start = (bf16[512,128]{1,0:T(8,128)(2,1)S(1)}, bf16[512,128]{1,0:T(8,128)(2,1)}, u32[]{:S(2)}) copy-start(bf16[512,128]{1,0:T(8,128)(2,1)} %param.8) | copy-start | bytes 393220
  8.0 44.5 %copy-start.1 = (bf16[128,128]{1,0:T(8,128)(2,1)S(1)}, bf16[128,128]{1,0:T(8,128)(2,1)}, u32[]{:S(2)}) copy-start(bf16[128,128]{1,0:T(8,128)(2,1)} %param.13) | copy-start | bytes 98308
  8.0 64.4 %reduce-scatter.2.cloned.1.call-start = ((), (), s32[]{:S(2)}) async-start(), calls=%async_computation.1 | async-start | bytes 327680 | tf_op jit(solution)/shard_map/reduce_scatter | solution.py:66
  28.5 25.9 %copy-start.2 = (u32[32]{0:T(128)S(1)}, u32[32]{0:T(128)}, u32[]{:S(2)}) copy-start(u32[32]{0:T(128)} %constant.35) | copy-start | bytes 388
  53.5 31.1 %all-gather.7.cloned.1.call-start = ((), (), s32[]{:S(2)}) async-start(), calls=%async_computation.2 | async-start | bytes 2359296 | tf_op jit(solution)/shard_map/all_gather | solution.py:61
Sparse Core Ops, SparseCore 0:
  53.6 18.7 reduce-scatter.1
Sparse Core Ops, SparseCore 1:
  56.4 27.9 all-gather.6
